TPU v7x, 32 devices: a whole 2x2x4 slice. The times are simulated.
32 devices in a mesh: elem: 2 (over core), band: 16 (over z, y, x).
Axes of the slice: x: 2, y: 2, z: 4, core: 2. Of those that a mesh axis runs over, the one named last changes fastest.
Arguments:
- coefficients: bfloat16 [8, 128, 8192], P('elem', None, 'band'), may hold values from -6 to 6
- hamiltonian: bfloat16 [8, 27, 128, 128], P('elem'), may hold values from -0.0546875 to 0.0546875
- neighbours: int32 [8, 27], P('elem'), may hold values from 0 to 7, as said below
- basis_values: bfloat16 [8, 4096, 128], P('elem'), may hold values from -0.5 to 0.5
Outputs:
- filtered: bfloat16 [8, 128, 8192], P('elem', None, 'band')
- density: float32 [8, 4096], P('elem', 'band')
Inputs may be any that keep to these rules, and one draw needn't show every extreme that they name: `neighbours`: elements sit on a periodic grid of 2 x 2 x 2 cells in an order drawn from the seed; row e lists the elements at offsets (dx, dy, dz) in -1..1, with k = 9 (dx + 1) + 3 (dy + 1) + dz + 1.
All inputs are finite; a program needn't handle non-finite values.
Results may differ from a plain program's by a relative error of at most 0.0065.
Values may be sent and summed in bfloat16 or wider, within the bound.
A program may use at most 64 MiB of HBM per device.

v0:
```python
import functools

import jax
import jax.numpy as jnp
from jax import lax
from jax.experimental import pallas as pl
from jax.experimental.pallas import tpu as pltpu
from jax.sharding import PartitionSpec as P

CHEB = 6
OFFSETS = 27
MESH = pl.DeviceIdType.MESH


def classes_of(folded):
    groups = {}
    for k in range(OFFSETS):
        shift = (k // 9 - 1, k // 3 % 3 - 1, k % 3 - 1)
        key = tuple(s % 2 if f else s + 1 for s, f in zip(shift, folded))
        groups.setdefault(key, []).append(k)
    return [groups[key] for key in sorted(groups)]


def plain(coefficients, hamiltonian, neighbours, basis_values, bands):
    groups = classes_of((False, True, True))
    wide = hamiltonian.astype(jnp.float32)
    blocks = jnp.stack([sum(wide[:, k] for k in g) for g in groups], axis=1).astype(jnp.bfloat16)
    index = jnp.stack([neighbours[:, g[0]] for g in groups], axis=1)

    def apply_operator(current):
        everyone = lax.all_gather(current, "elem", axis=0, tiled=True)
        return jnp.einsum("ekij,ekjb->eib", blocks, everyone[index], preferred_element_type=jnp.float32)

    previous = coefficients.astype(jnp.float32)
    current = apply_operator(coefficients)
    for _ in range(CHEB - 1):
        following = 2.0 * apply_operator(current.astype(jnp.bfloat16)) - previous
        previous, current = current, following
    filtered = current.astype(jnp.bfloat16)
    orbital = jnp.einsum("epj,ejb->epb", basis_values, filtered, preferred_element_type=jnp.float32)
    terms = jnp.sum(orbital * orbital, axis=2)
    summed = lax.psum_scatter(terms, "band", scatter_dimension=1, tiled=True)
    return filtered, summed / bands


def fused(peers, bands, plane, nb_ref, c_hbm, h_hbm, b_hbm, f_ref, d_ref,
          hraw, hsum, hd, y0, y1, z0, z1, fsend, fown, frecv, basis, gblock, part, rbuf,
          hello, ready, load_sem, c_send, c_recv, h_send, h_recv, f_send, f_recv, d_send, d_recv):
    me = lax.axis_index("elem")
    mine = lax.axis_index("band")
    other = 1 - me
    local, nb, width = c_hbm.shape
    half = width // 2
    elems = 2 * local
    points = b_hbm.shape[1] // peers

    my_rows = pl.ds(me * local, local)
    other_rows = pl.ds(other * local, local)
    my_bands = pl.ds(pl.multiple_of(me * half, half), half)
    other_bands = pl.ds(pl.multiple_of(other * half, half), half)

    loads = [pltpu.make_async_copy(h_hbm.at[e], hraw.at[e], load_sem.at[e]) for e in range(local)]
    for copy in loads:
        copy.start()
    c_load = pltpu.make_async_copy(c_hbm.at[:, :, my_bands], y0.at[my_rows], load_sem.at[local])
    c_load.start()
    b_loads = [pltpu.make_async_copy(b_hbm.at[e], basis.at[e // 2, :, pl.ds(e % 2 * nb, nb)], load_sem.at[local + 1 + e]) for e in range(local)]
    for copy in b_loads:
        copy.start()

    barrier = pltpu.get_barrier_semaphore()

    @pl.when(me == 1)
    def _():
        pl.semaphore_signal(barrier, inc=1, device_id=(0, mine), device_id_type=MESH)

    @pl.when(me == 0)
    def _():
        pl.semaphore_wait(barrier, 1)
        pl.semaphore_signal(hello, inc=1, device_id=(1, mine), device_id_type=MESH)

    @pl.when(me == 1)
    def _():
        pl.semaphore_wait(hello, 1)

    c_copy = pltpu.make_async_remote_copy(
        src_ref=c_hbm.at[:, :, other_bands], dst_ref=y0.at[my_rows],
        send_sem=c_send, recv_sem=c_recv, device_id=(other, mine), device_id_type=MESH)
    c_copy.start()

    @pl.when(me == 1)
    def _():
        for i in range(1, peers):
            pl.semaphore_signal(barrier, inc=1, device_id=(1, lax.rem(mine + i, peers)), device_id_type=MESH)

    groups = classes_of((True, True, True))
    n = len(groups)

    def place(g):
        total = 0
        for c in range(1, n):
            total = total + jnp.where(nb_ref[0, groups[c][0]] == g, c, 0)
        return lax.rem(total, n)

    spots = [place(g) for g in range(elems)]

    def collapse(e):
        loads[e].wait()
        for c, group in enumerate(groups):
            total = hraw[e, group[0]].astype(jnp.float32)
            for k in group[1:]:
                total = total + hraw[e, k].astype(jnp.float32)
            hsum[e, c] = (total + total).astype(jnp.bfloat16)
        mine_spot = place(me * local + e)
        for g in range(elems):
            hd[me * local + e, :, g * nb:(g + 1) * nb] = hsum[e, mine_spot ^ spots[g]]

    h_copies = []
    for e in range(local):
        collapse(e)
        copy = pltpu.make_async_remote_copy(
            src_ref=hd.at[me * local + e], dst_ref=hd.at[me * local + e],
            send_sem=h_send.at[e], recv_sem=h_recv.at[e], device_id=(other, mine), device_id_type=MESH)
        copy.start()
        h_copies.append(copy)
    c_load.wait()
    c_copy.wait_recv()

    y, z = (y0, y1), (z0, z1)

    def product(source, at, count):
        left = hd[at].reshape(count * nb, elems * nb)
        right = y[source][...].reshape(elems * nb, half)
        out = jnp.dot(left, right, preferred_element_type=jnp.float32)
        return out.reshape(count, nb, half)

    for which in (my_rows, other_rows):
        if which is other_rows:
            for copy in h_copies:
                copy.wait_recv()
        first = 0.5 * product(0, which, local)
        z1[which] = first
        y1[which] = first.astype(jnp.bfloat16)
    for step in range(1, CHEB - 1):
        now, later = step % 2, (step + 1) % 2
        for which in (slice(0, local), slice(local, elems)):
            before = y0[which].astype(jnp.float32) if step == 1 else z[later][which]
            following = product(now, which, local) - before
            if step < CHEB - 2:
                z[later][which] = following
            y[later][which] = following.astype(jnp.bfloat16)

    now, later = (CHEB - 1) % 2, CHEB % 2
    fsend[...] = (product(now, other_rows, local) - z[later][other_rows]).astype(jnp.bfloat16)
    f_copy = pltpu.make_async_remote_copy(
        src_ref=fsend, dst_ref=frecv, send_sem=f_send, recv_sem=f_recv,
        device_id=(other, mine), device_id_type=MESH)
    f_copy.start()
    fown[...] = (product(now, my_rows, local) - z[later][my_rows]).astype(jnp.bfloat16)
    f_ref[:, :, my_bands] = fown[...]

    def gram(block):
        return lax.dot_general(block, block, (((1,), (1,)), ((), ())), preferred_element_type=jnp.float32)

    grams = [gram(fown[e]) for e in range(local)]
    gblock[...] = jnp.zeros(gblock.shape, gblock.dtype)
    for copy in b_loads:
        copy.wait()
    f_copy.wait_recv()
    f_ref[:, :, other_bands] = frecv[...]
    for e in range(local):
        at = pl.ds(e % 2 * nb, nb)
        gblock[e // 2, at, at] = (grams[e] + gram(frecv[e])).astype(jnp.bfloat16)
    pick = (lax.broadcasted_iota(jnp.int32, (8, 2 * nb), 0)
            == lax.broadcasted_iota(jnp.int32, (8, 2 * nb), 1) // nb).astype(jnp.bfloat16)

    def terms(group):
        size = plane * points
        at = pl.ds(pl.multiple_of(group * size, size), size)
        for pair in range(local // 2):
            values = basis[pair, at]
            moved = jnp.dot(values, gblock[pair], preferred_element_type=jnp.float32)
            products = moved * values.astype(jnp.float32)
            if pair % 2:
                sums = lax.dot_general(pick, products.astype(jnp.bfloat16), (((1,), (1,)), ((), ())),
                                       preferred_element_type=jnp.float32)
                for q in range(plane):
                    part[group * plane + q, 2 * pair:2 * pair + 2] = sums[:2, q * points:(q + 1) * points]
                continue
            for k in range(2):
                sums = jnp.sum(products[:, k * nb:(k + 1) * nb].reshape(size // 128, 128, nb), axis=2)
                for r in range(size // 128):
                    q, column = r * 128 // points, r * 128 % points
                    part[group * plane + q, 2 * pair + k:2 * pair + k + 1, column:column + 128] = sums[r:r + 1]

    def d_copy(i):
        target = lax.rem(mine + i, peers)
        return pltpu.make_async_remote_copy(
            src_ref=part.at[target], dst_ref=rbuf.at[i], send_sem=d_send.at[i], recv_sem=d_recv.at[i],
            device_id=(me, target), device_id_type=MESH)

    @pl.when(me == 1)
    def _():
        pl.semaphore_wait(barrier, peers - 1)
        pl.semaphore_signal(ready, inc=1, device_id=(0, mine), device_id_type=MESH)

    @pl.when(me == 0)
    def _():
        pl.semaphore_wait(ready, 1)

    planes = peers // plane
    for away in sorted(range(planes), key=lambda a: -min(a, planes - a)):
        group = lax.rem(mine // plane + away, planes)
        terms(group)
        for d in range(0 if away else 1, plane):
            target = group * plane + lax.rem(mine + d, plane)
            d_copy(lax.rem(target - mine + peers, peers)).start()
    total = part[mine]
    for i in range(1, peers):
        d_copy(i).wait_recv()
        total = total + rbuf[i]
    d_ref[...] = total / bands

    for i in range(1, peers):
        d_copy(i).wait_send()
    c_copy.wait_send()
    for copy in h_copies:
        copy.wait_send()
    f_copy.wait_send()


def deliver(f_in, d_in, f_hbm, d_ref, sem):
    copy = pltpu.make_async_copy(f_in, f_hbm, sem)
    copy.start()
    d_ref[...] = d_in[...]
    copy.wait()


def quick(coefficients, hamiltonian, neighbours, basis_values, peers, bands):
    local, nb, width = coefficients.shape
    half = width // 2
    elems = 2 * local
    points = basis_values.shape[1]
    share = points // peers
    plane = 4 if peers % 4 == 0 else 1
    bf16, f32, dma = jnp.bfloat16, jnp.float32, pltpu.SemaphoreType.DMA
    grant = 67043328 - 2 * local * nb * width - 4 * local * share
    filtered, density = pl.pallas_call(
        functools.partial(fused, peers, bands, plane),
        out_shape=(pltpu.VMEM((local, nb, width), bf16), pltpu.VMEM((local, share), f32)),
        in_specs=[pl.BlockSpec(memory_space=pltpu.SMEM)] + [pl.BlockSpec(memory_space=pltpu.HBM)] * 3,
        out_specs=(pl.BlockSpec(memory_space=pltpu.VMEM), pl.BlockSpec(memory_space=pltpu.VMEM)),
        scratch_shapes=[
            pltpu.VMEM((local, OFFSETS, nb, nb), bf16),
            pltpu.VMEM((local, 8, nb, nb), bf16),
            pltpu.VMEM((elems, nb, elems * nb), bf16),
            pltpu.VMEM((elems, nb, half), bf16),
            pltpu.VMEM((elems, nb, half), bf16),
            pltpu.VMEM((elems, nb, half), f32),
            pltpu.VMEM((elems, nb, half), f32),
            pltpu.VMEM((local, nb, half), bf16),
            pltpu.VMEM((local, nb, half), bf16),
            pltpu.VMEM((local, nb, half), bf16),
            pltpu.VMEM((local // 2, points, 2 * nb), bf16),
            pltpu.VMEM((local // 2, 2 * nb, 2 * nb), bf16),
            pltpu.VMEM((peers, local, share), f32),
            pltpu.VMEM((peers, local, share), f32),
            pltpu.SemaphoreType.REGULAR, pltpu.SemaphoreType.REGULAR,
            dma((2 * local + 1,)),
            dma, dma,
            dma((local,)), dma((local,)),
            dma, dma,
            dma((peers,)), dma((peers,)),
        ],
        compiler_params=pltpu.CompilerParams(
            collective_id=0, has_side_effects=True, vmem_limit_bytes=grant),
    )(neighbours, coefficients, hamiltonian, basis_values)
    return pl.pallas_call(
        deliver,
        out_shape=(jax.ShapeDtypeStruct((local, nb, width), bf16), jax.ShapeDtypeStruct((local, share), f32)),
        in_specs=[pl.BlockSpec(memory_space=pltpu.VMEM)] * 2,
        out_specs=(pl.BlockSpec(memory_space=pl.ANY), pl.BlockSpec(memory_space=pltpu.VMEM)),
        scratch_shapes=[dma],
        compiler_params=pltpu.CompilerParams(vmem_limit_bytes=4 * 2**20),
    )(filtered, density)


def solution(mesh):
    split, peers = mesh.shape["elem"], mesh.shape["band"]

    def local(coefficients, hamiltonian, neighbours, basis_values):
        count, nb, width = coefficients.shape
        bands = width * peers
        fits = (split == 2 and count * split == 8 and nb == 128 and width % 256 == 0
                and basis_values.shape[1] % (128 * peers) == 0)
        if fits:
            return quick(coefficients, hamiltonian, neighbours, basis_values, peers, bands)
        return plain(coefficients, hamiltonian, neighbours, basis_values, bands)

    return jax.shard_map(
        local,
        mesh=mesh,
        in_specs=(
            P("elem", None, "band"),
            P("elem", None, None, None),
            P("elem", None),
            P("elem", None, None),
        ),
        out_specs=(P("elem", None, "band"), P("elem", "band")),
        check_vma=False,
    )
```

profile of v0, /device:TPU:0, one launch (start us, length us, event | category | flops | bytes accessed | tf_op | source)
XLA Modules:
  0.0 22.1 jit_solution(3474185703522309723)
XLA Ops:
  0.6 20.1 %shard_map.59 = (bf16[4,128,512]{2,1,0:T(8,128)(2,1)S(1)}, f32[4,256]{1,0:T(4,128)S(1)}) custom-call(s32[4,27]{1,0:T(4,128)} %nb_ref.1, bf16[4,128,512]{2,1,0:T(8,128)(2,1)} %c_hbm.1, bf16[4,27,128,128]{3,2,1,0:T(8,128)(2,1)} %h_hbm.1, bf16[4,4096,128]{2,1,0:T(8,128)(2,1)} %b_hbm.1), custom_call_target="tpu_custom_call" | custom-call | tf_op jit(solution)/shard_map/pallas_call | solution.py:248
  20.7 1.4 %shard_map.60 = (bf16[4,128,512]{2,1,0:T(8,128)(2,1)}, f32[4,256]{1,0:T(4,128)}) custom-call(bf16[4,128,512]{2,1,0:T(8,128)(2,1)S(1)} %get-tuple-element.4.f_in, f32[4,256]{1,0:T(4,128)S(1)} %get-tuple-element.5.d_in), custom_call_target="tpu_custom_call" | custom-call | tf_op jit(solution)/shard_map/pallas_call | solution.py:278
where the time goes:
time: 22.3 us; the launch traced here: 22.1 us
  Pallas kernels  21.5 us (96%)
  between operations  0.64 us (3%)
    pallas_call x1, Pallas kernels, quick(): pl.pallas_call(functools.partial(fused, peers, bands, plane), out_shape=(...  20.1 us
    pallas_call x1, Pallas kernels, quick(): pl.pallas_call(deliver, out_shape=(jax.ShapeDtypeStruct((local, nb, width...  1.4 us

commit v1 on v0

--- a/solution.py
+++ b/solution.py
@@ -9,6 +9,7 @@
 
 CHEB = 6
 OFFSETS = 27
+STEP = 2
 MESH = pl.DeviceIdType.MESH
 
 
@@ -43,9 +44,9 @@
     return filtered, summed / bands
 
 
-def fused(peers, bands, plane, nb_ref, c_hbm, h_hbm, b_hbm, f_ref, d_ref,
-          hraw, hsum, hd, y0, y1, z0, z1, fsend, fown, frecv, basis, gblock, part, rbuf,
-          hello, ready, load_sem, c_send, c_recv, h_send, h_recv, f_send, f_recv, d_send, d_recv):
+def fused(peers, bands, plane, nb_hbm, c_hbm, h_hbm, b_hbm, f_ref, d_ref,
+          hraw, hsum, hd, y0, y1, z0, z1, fsend, fown, frecv, basis, gblock, part, early, rbuf, nb_ref,
+          hello, ready, nb_sem, load_sem, c_send, c_recv, h_send, h_recv, f_send, f_recv, d_send, d_recv):
     me = lax.axis_index("elem")
     mine = lax.axis_index("band")
     other = 1 - me
@@ -60,7 +61,10 @@
     other_bands = pl.ds(pl.multiple_of(other * half, half), half)
 
     loads = [pltpu.make_async_copy(h_hbm.at[e], hraw.at[e], load_sem.at[e]) for e in range(local)]
-    for copy in loads:
+    loads[0].start()
+    nb_load = pltpu.make_async_copy(nb_hbm, nb_ref, nb_sem)
+    nb_load.start()
+    for copy in loads[1:]:
         copy.start()
     c_load = pltpu.make_async_copy(c_hbm.at[:, :, my_bands], y0.at[my_rows], load_sem.at[local])
     c_load.start()
@@ -102,6 +106,7 @@
             total = total + jnp.where(nb_ref[0, groups[c][0]] == g, c, 0)
         return lax.rem(total, n)
 
+    nb_load.wait()
     spots = [place(g) for g in range(elems)]
 
     def collapse(e):
@@ -134,13 +139,17 @@
         out = jnp.dot(left, right, preferred_element_type=jnp.float32)
         return out.reshape(count, nb, half)
 
-    for which in (my_rows, other_rows):
-        if which is other_rows:
-            for copy in h_copies:
-                copy.wait_recv()
-        first = 0.5 * product(0, which, local)
-        z1[which] = first
-        y1[which] = first.astype(jnp.bfloat16)
+    def begin(at, count):
+        rows = pl.ds(at, count)
+        first = 0.5 * product(0, rows, count)
+        z1[rows] = first
+        y1[rows] = first.astype(jnp.bfloat16)
+
+    begin(me * local, local)
+    for e in range(0, local, STEP):
+        for copy in h_copies[e:e + STEP]:
+            copy.wait_recv()
+        begin(other * local + e, STEP)
     for step in range(1, CHEB - 1):
         now, later = step % 2, (step + 1) % 2
         for which in (slice(0, local), slice(local, elems)):
@@ -174,9 +183,8 @@
     pick = (lax.broadcasted_iota(jnp.int32, (8, 2 * nb), 0)
             == lax.broadcasted_iota(jnp.int32, (8, 2 * nb), 1) // nb).astype(jnp.bfloat16)
 
-    def terms(group):
-        size = plane * points
-        at = pl.ds(pl.multiple_of(group * size, size), size)
+    def terms(start, size, store):
+        at = pl.ds(start, size)
         for pair in range(local // 2):
             values = basis[pair, at]
             moved = jnp.dot(values, gblock[pair], preferred_element_type=jnp.float32)
@@ -184,19 +192,30 @@
             if pair % 2:
                 sums = lax.dot_general(pick, products.astype(jnp.bfloat16), (((1,), (1,)), ((), ())),
                                        preferred_element_type=jnp.float32)
-                for q in range(plane):
-                    part[group * plane + q, 2 * pair:2 * pair + 2] = sums[:2, q * points:(q + 1) * points]
+                for column in range(0, size, points):
+                    store(column, slice(2 * pair, 2 * pair + 2), slice(0, points), sums[:2, column:column + points])
                 continue
             for k in range(2):
                 sums = jnp.sum(products[:, k * nb:(k + 1) * nb].reshape(size // 128, 128, nb), axis=2)
                 for r in range(size // 128):
-                    q, column = r * 128 // points, r * 128 % points
-                    part[group * plane + q, 2 * pair + k:2 * pair + k + 1, column:column + 128] = sums[r:r + 1]
-
-    def d_copy(i):
+                    column = r * 128 // points * points
+                    store(column, slice(2 * pair + k, 2 * pair + k + 1),
+                          slice(r * 128 - column, r * 128 - column + 128), sums[r:r + 1])
+
+    def group_terms(group):
+        def store(column, rows, columns, value):
+            part[group * plane + column // points, rows, columns] = value
+        terms(pl.multiple_of(group * plane * points, plane * points), plane * points, store)
+
+    def early_terms():
+        def store(column, rows, columns, value):
+            early[rows, columns] = value
+        terms(0, points, store)
+
+    def d_copy(i, source=None):
         target = lax.rem(mine + i, peers)
         return pltpu.make_async_remote_copy(
-            src_ref=part.at[target], dst_ref=rbuf.at[i], send_sem=d_send.at[i], recv_sem=d_recv.at[i],
+            src_ref=part.at[target] if source is None else source, dst_ref=rbuf.at[i], send_sem=d_send.at[i], recv_sem=d_recv.at[i],
             device_id=(me, target), device_id_type=MESH)
 
     @pl.when(me == 1)
@@ -208,13 +227,25 @@
     def _():
         pl.semaphore_wait(ready, 1)
 
+    early_terms()
+
+    @pl.when(mine != 0)
+    def _():
+        d_copy(peers - mine, early).start()
+
     planes = peers // plane
-    for away in sorted(range(planes), key=lambda a: -min(a, planes - a)):
-        group = lax.rem(mine // plane + away, planes)
-        terms(group)
-        for d in range(0 if away else 1, plane):
+    own = mine // plane
+    for turn in range(planes):
+        up = jnp.where(turn < planes - 1 - own, planes - 1 - turn, turn - (planes - 1 - own))
+        down = jnp.where(turn < own, turn, planes - 1 - (turn - own))
+        group = own if turn == planes - 1 else jnp.where(2 * own < planes, up, down)
+        group_terms(group)
+        for d in range(1 if turn == planes - 1 else 0, plane):
             target = group * plane + lax.rem(mine + d, plane)
-            d_copy(lax.rem(target - mine + peers, peers)).start()
+
+            @pl.when(target != 0)
+            def _(target=target):
+                d_copy(lax.rem(target - mine + peers, peers)).start()
     total = part[mine]
     for i in range(1, peers):
         d_copy(i).wait_recv()
@@ -229,11 +260,12 @@
     f_copy.wait_send()
 
 
-def deliver(f_in, d_in, f_hbm, d_ref, sem):
-    copy = pltpu.make_async_copy(f_in, f_hbm, sem)
-    copy.start()
-    d_ref[...] = d_in[...]
-    copy.wait()
+def deliver(f_in, d_in, f_hbm, d_hbm, sem):
+    copies = [pltpu.make_async_copy(f_in, f_hbm, sem.at[0]), pltpu.make_async_copy(d_in, d_hbm, sem.at[1])]
+    for copy in copies:
+        copy.start()
+    for copy in copies:
+        copy.wait()
 
 
 def quick(coefficients, hamiltonian, neighbours, basis_values, peers, bands):
@@ -248,7 +280,7 @@
     filtered, density = pl.pallas_call(
         functools.partial(fused, peers, bands, plane),
         out_shape=(pltpu.VMEM((local, nb, width), bf16), pltpu.VMEM((local, share), f32)),
-        in_specs=[pl.BlockSpec(memory_space=pltpu.SMEM)] + [pl.BlockSpec(memory_space=pltpu.HBM)] * 3,
+        in_specs=[pl.BlockSpec(memory_space=pltpu.HBM)] * 4,
         out_specs=(pl.BlockSpec(memory_space=pltpu.VMEM), pl.BlockSpec(memory_space=pltpu.VMEM)),
         scratch_shapes=[
             pltpu.VMEM((local, OFFSETS, nb, nb), bf16),
@@ -264,8 +296,11 @@
             pltpu.VMEM((local // 2, points, 2 * nb), bf16),
             pltpu.VMEM((local // 2, 2 * nb, 2 * nb), bf16),
             pltpu.VMEM((peers, local, share), f32),
+            pltpu.VMEM((local, share), f32),
             pltpu.VMEM((peers, local, share), f32),
+            pltpu.SMEM(neighbours.shape, jnp.int32),
             pltpu.SemaphoreType.REGULAR, pltpu.SemaphoreType.REGULAR,
+            dma,
             dma((2 * local + 1,)),
             dma, dma,
             dma((local,)), dma((local,)),
@@ -279,8 +314,8 @@
         deliver,
         out_shape=(jax.ShapeDtypeStruct((local, nb, width), bf16), jax.ShapeDtypeStruct((local, share), f32)),
         in_specs=[pl.BlockSpec(memory_space=pltpu.VMEM)] * 2,
-        out_specs=(pl.BlockSpec(memory_space=pl.ANY), pl.BlockSpec(memory_space=pltpu.VMEM)),
-        scratch_shapes=[dma],
+        out_specs=(pl.BlockSpec(memory_space=pl.ANY), pl.BlockSpec(memory_space=pl.ANY)),
+        scratch_shapes=[dma((2,))],
         compiler_params=pltpu.CompilerParams(vmem_limit_bytes=4 * 2**20),
     )(filtered, density)
 

time: 22.3 us -> 19.9 us (0.89)
  Pallas kernels: 21.5 us -> 19.1 us
    pallas_call x1, Pallas kernels: 20.1 us -> 18.3 us  [quick(): pl.pallas_call(functools.partial(fused, peers, bands, plane), out_shape=(...]
    pallas_call x1, Pallas kernels: 1.4 us -> 0.81 us  [quick(): pl.pallas_call(deliver, out_shape=(jax.ShapeDtypeStruct((local, nb, width...]
where the time goes in v1:
time: 19.9 us; the launch traced here: 19.7 us
  Pallas kernels  19.1 us (96%)
  between operations  0.64 us (3%)
    pallas_call x1, Pallas kernels, quick(): pl.pallas_call(functools.partial(fused, peers, bands, plane), out_shape=(...  18.3 us
    pallas_call x1, Pallas kernels, quick(): pl.pallas_call(deliver, out_shape=(jax.ShapeDtypeStruct((local, nb, width...  0.81 us

profile of v1, /device:TPU:0, one launch (start us, length us, event | category | flops | bytes accessed | tf_op | source)
XLA Modules:
  0.0 19.7 jit_solution(5843633889575489355)
XLA Ops:
  0.6 18.3 %shard_map.59 = (bf16[4,128,512]{2,1,0:T(8,128)(2,1)S(1)}, f32[4,256]{1,0:T(4,128)S(1)}) custom-call(s32[4,27]{1,0:T(4,128)} %nb_hbm.1, bf16[4,128,512]{2,1,0:T(8,128)(2,1)} %c_hbm.1, bf16[4,27,128,128]{3,2,1,0:T(8,128)(2,1)} %h_hbm.1, bf16[4,4096,128]{2,1,0:T(8,128)(2,1)} %b_hbm.1), custom_call_target="tpu_custom_call" | custom-call | tf_op jit(solution)/shard_map/pallas_call | solution.py:280
  18.9 0.8 %shard_map.60 = (bf16[4,128,512]{2,1,0:T(8,128)(2,1)}, f32[4,256]{1,0:T(4,128)}) custom-call(bf16[4,128,512]{2,1,0:T(8,128)(2,1)S(1)} %get-tuple-element.4.f_in, f32[4,256]{1,0:T(4,128)S(1)} %get-tuple-element.5.d_in), custom_call_target="tpu_custom_call" | custom-call | tf_op jit(solution)/shard_map/pallas_call | solution.py:313

commit v2 on v1

--- a/solution.py
+++ b/solution.py
@@ -10,6 +10,7 @@
 CHEB = 6
 OFFSETS = 27
 STEP = 2
+SPLIT = 2
 MESH = pl.DeviceIdType.MESH
 
 
@@ -20,6 +21,10 @@
         key = tuple(s % 2 if f else s + 1 for s, f in zip(shift, folded))
         groups.setdefault(key, []).append(k)
     return [groups[key] for key in sorted(groups)]
+
+
+def chunks_of(local, nb):
+    return [(e, at, nb // n) for e in range(local) for n in [SPLIT if e == 0 else 1] for at in range(0, nb, nb // n)]
 
 
 def plain(coefficients, hamiltonian, neighbours, basis_values, bands):
@@ -45,8 +50,9 @@
 
 
 def fused(peers, bands, plane, nb_hbm, c_hbm, h_hbm, b_hbm, f_ref, d_ref,
-          hraw, hsum, hd, y0, y1, z0, z1, fsend, fown, frecv, basis, gblock, part, early, rbuf, nb_ref,
-          hello, ready, nb_sem, load_sem, c_send, c_recv, h_send, h_recv, f_send, f_recv, d_send, d_recv):
+          hraw, hsum, hd, y0, y1, z0, z1, fall, frecv, basis, near, gblock, part, early, rbuf, ebuf, nb_ref,
+          hello, ready, nb_sem, load_sem, c_send, c_recv, h_load, h_send, h_recv, f_send, f_recv, t_send, t_recv,
+          d_send, d_recv, e_send, e_recv):
     me = lax.axis_index("elem")
     mine = lax.axis_index("band")
     other = 1 - me
@@ -60,7 +66,9 @@
     my_bands = pl.ds(pl.multiple_of(me * half, half), half)
     other_bands = pl.ds(pl.multiple_of(other * half, half), half)
 
-    loads = [pltpu.make_async_copy(h_hbm.at[e], hraw.at[e], load_sem.at[e]) for e in range(local)]
+    cuts = chunks_of(local, nb)
+    loads = [pltpu.make_async_copy(h_hbm.at[e, :, pl.ds(at, rows)], hraw.at[e, :, pl.ds(at, rows)], h_load.at[i])
+             for i, (e, at, rows) in enumerate(cuts)]
     loads[0].start()
     nb_load = pltpu.make_async_copy(nb_hbm, nb_ref, nb_sem)
     nb_load.start()
@@ -69,8 +77,6 @@
     c_load = pltpu.make_async_copy(c_hbm.at[:, :, my_bands], y0.at[my_rows], load_sem.at[local])
     c_load.start()
     b_loads = [pltpu.make_async_copy(b_hbm.at[e], basis.at[e // 2, :, pl.ds(e % 2 * nb, nb)], load_sem.at[local + 1 + e]) for e in range(local)]
-    for copy in b_loads:
-        copy.start()
 
     barrier = pltpu.get_barrier_semaphore()
 
@@ -109,25 +115,34 @@
     nb_load.wait()
     spots = [place(g) for g in range(elems)]
 
-    def collapse(e):
-        loads[e].wait()
+    def collapse(i, e, at, rows):
+        loads[i].wait()
+        here = slice(at, at + rows)
         for c, group in enumerate(groups):
-            total = hraw[e, group[0]].astype(jnp.float32)
+            total = hraw[e, group[0], here].astype(jnp.float32)
             for k in group[1:]:
-                total = total + hraw[e, k].astype(jnp.float32)
-            hsum[e, c] = (total + total).astype(jnp.bfloat16)
+                total = total + hraw[e, k, here].astype(jnp.float32)
+            hsum[e, c, here] = (total + total).astype(jnp.bfloat16)
         mine_spot = place(me * local + e)
         for g in range(elems):
-            hd[me * local + e, :, g * nb:(g + 1) * nb] = hsum[e, mine_spot ^ spots[g]]
+            hd[me * local + e, here, g * nb:(g + 1) * nb] = hsum[e, mine_spot ^ spots[g], here]
 
     h_copies = []
-    for e in range(local):
-        collapse(e)
+    for i, (e, at, rows) in enumerate(cuts):
+        collapse(i, e, at, rows)
         copy = pltpu.make_async_remote_copy(
-            src_ref=hd.at[me * local + e], dst_ref=hd.at[me * local + e],
-            send_sem=h_send.at[e], recv_sem=h_recv.at[e], device_id=(other, mine), device_id_type=MESH)
+            src_ref=hd.at[me * local + e, pl.ds(at, rows)], dst_ref=hd.at[me * local + e, pl.ds(at, rows)],
+            send_sem=h_send.at[i], recv_sem=h_recv.at[i], device_id=(other, mine), device_id_type=MESH)
         copy.start()
         h_copies.append(copy)
+    for copy in b_loads:
+        copy.start()
+    t_copy = pltpu.make_async_remote_copy(
+        src_ref=b_hbm.at[:, pl.ds(0, points)], dst_ref=near.at[my_rows],
+        send_sem=t_send, recv_sem=t_recv, device_id=(other, mine), device_id_type=MESH)
+    t_copy.start()
+    n_load = pltpu.make_async_copy(b_hbm.at[:, pl.ds(0, points)], near.at[my_rows], load_sem.at[2 * local + 1])
+    n_load.start()
     c_load.wait()
     c_copy.wait_recv()
 
@@ -147,8 +162,9 @@
 
     begin(me * local, local)
     for e in range(0, local, STEP):
-        for copy in h_copies[e:e + STEP]:
-            copy.wait_recv()
+        for copy, cut in zip(h_copies, cuts):
+            if e <= cut[0] < e + STEP:
+                copy.wait_recv()
         begin(other * local + e, STEP)
     for step in range(1, CHEB - 1):
         now, later = step % 2, (step + 1) % 2
@@ -159,79 +175,100 @@
                 z[later][which] = following
             y[later][which] = following.astype(jnp.bfloat16)
 
+    def early_terms(side):
+        for e in range(local):
+            orbital = jnp.dot(near[side * local + e], fall[side * local + e], preferred_element_type=jnp.float32)
+            squares = sum(orbital[:, at:at + 128] * orbital[:, at:at + 128] for at in range(0, half, 128))
+            sums = jnp.sum(squares.reshape(points // 128, 128, 128), axis=2)
+            for r in range(points // 128):
+                early[side, e:e + 1, r * 128:(r + 1) * 128] = sums[r:r + 1]
+
+    def e_copy(side):
+        slot = lax.rem(me + side, 2) * peers + mine
+        copy = pltpu.make_async_remote_copy(
+            src_ref=early.at[side], dst_ref=ebuf.at[slot], send_sem=e_send.at[side], recv_sem=e_recv,
+            device_id=(side, 0), device_id_type=MESH)
+        return slot != 0, copy
+
+    @pl.when(me == 1)
+    def _():
+        pl.semaphore_wait(barrier, peers - 1)
+        pl.semaphore_signal(ready, inc=1, device_id=(0, mine), device_id_type=MESH)
+
+    @pl.when(me == 0)
+    def _():
+        pl.semaphore_wait(ready, 1)
+
+    t_copy.wait_recv()
+    n_load.wait()
     now, later = (CHEB - 1) % 2, CHEB % 2
-    fsend[...] = (product(now, other_rows, local) - z[later][other_rows]).astype(jnp.bfloat16)
     f_copy = pltpu.make_async_remote_copy(
-        src_ref=fsend, dst_ref=frecv, send_sem=f_send, recv_sem=f_recv,
+        src_ref=fall.at[other_rows], dst_ref=frecv, send_sem=f_send, recv_sem=f_recv,
         device_id=(other, mine), device_id_type=MESH)
-    f_copy.start()
-    fown[...] = (product(now, my_rows, local) - z[later][my_rows]).astype(jnp.bfloat16)
-    f_ref[:, :, my_bands] = fown[...]
+    for side in range(2):
+        which = slice(side * local, (side + 1) * local)
+        fall[which] = (product(now, which, local) - z[later][which]).astype(jnp.bfloat16)
+
+        @pl.when(me != side)
+        def _():
+            f_copy.start()
+
+        early_terms(side)
+        sends, copy = e_copy(side)
+
+        @pl.when(sends)
+        def _(copy=copy):
+            copy.start()
+
+    f_ref[:, :, my_bands] = fall[my_rows]
 
     def gram(block):
         return lax.dot_general(block, block, (((1,), (1,)), ((), ())), preferred_element_type=jnp.float32)
 
-    grams = [gram(fown[e]) for e in range(local)]
-    gblock[...] = jnp.zeros(gblock.shape, gblock.dtype)
     for copy in b_loads:
         copy.wait()
+    grams = [gram(fall[me * local + e]) for e in range(local)]
+    gblock[...] = jnp.zeros(gblock.shape, gblock.dtype)
+    pick = (lax.broadcasted_iota(jnp.int32, (8, 2 * nb), 0)
+            == lax.broadcasted_iota(jnp.int32, (8, 2 * nb), 1) // nb).astype(jnp.bfloat16)
+
+    def terms(values, block, pair, store):
+        size = values.shape[0]
+        moved = jnp.dot(values, block, preferred_element_type=jnp.float32)
+        products = moved * values.astype(jnp.float32)
+        if pair % 2:
+            sums = lax.dot_general(pick, products.astype(jnp.bfloat16), (((1,), (1,)), ((), ())),
+                                   preferred_element_type=jnp.float32)
+            for column in range(0, size, points):
+                store(column, slice(2 * pair, 2 * pair + 2), slice(0, points), sums[:2, column:column + points])
+            return
+        for k in range(2):
+            sums = jnp.sum(products[:, k * nb:(k + 1) * nb].reshape(size // 128, 128, nb), axis=2)
+            for r in range(size // 128):
+                column = r * 128 // points * points
+                store(column, slice(2 * pair + k, 2 * pair + k + 1),
+                      slice(r * 128 - column, r * 128 - column + 128), sums[r:r + 1])
+
+    def group_terms(group):
+        size = plane * points
+        at = pl.ds(pl.multiple_of(group * size, size), size)
+
+        def store(column, rows, columns, value):
+            part[group * plane + column // points, rows, columns] = value
+        for pair in range(local // 2):
+            terms(basis[pair, at], gblock[pair], pair, store)
+
+    def d_copy(i):
+        target = lax.rem(mine + i, peers)
+        return pltpu.make_async_remote_copy(
+            src_ref=part.at[target], dst_ref=rbuf.at[i], send_sem=d_send.at[i], recv_sem=d_recv.at[i],
+            device_id=(me, target), device_id_type=MESH)
+
     f_copy.wait_recv()
     f_ref[:, :, other_bands] = frecv[...]
     for e in range(local):
         at = pl.ds(e % 2 * nb, nb)
         gblock[e // 2, at, at] = (grams[e] + gram(frecv[e])).astype(jnp.bfloat16)
-    pick = (lax.broadcasted_iota(jnp.int32, (8, 2 * nb), 0)
-            == lax.broadcasted_iota(jnp.int32, (8, 2 * nb), 1) // nb).astype(jnp.bfloat16)
-
-    def terms(start, size, store):
-        at = pl.ds(start, size)
-        for pair in range(local // 2):
-            values = basis[pair, at]
-            moved = jnp.dot(values, gblock[pair], preferred_element_type=jnp.float32)
-            products = moved * values.astype(jnp.float32)
-            if pair % 2:
-                sums = lax.dot_general(pick, products.astype(jnp.bfloat16), (((1,), (1,)), ((), ())),
-                                       preferred_element_type=jnp.float32)
-                for column in range(0, size, points):
-                    store(column, slice(2 * pair, 2 * pair + 2), slice(0, points), sums[:2, column:column + points])
-                continue
-            for k in range(2):
-                sums = jnp.sum(products[:, k * nb:(k + 1) * nb].reshape(size // 128, 128, nb), axis=2)
-                for r in range(size // 128):
-                    column = r * 128 // points * points
-                    store(column, slice(2 * pair + k, 2 * pair + k + 1),
-                          slice(r * 128 - column, r * 128 - column + 128), sums[r:r + 1])
-
-    def group_terms(group):
-        def store(column, rows, columns, value):
-            part[group * plane + column // points, rows, columns] = value
-        terms(pl.multiple_of(group * plane * points, plane * points), plane * points, store)
-
-    def early_terms():
-        def store(column, rows, columns, value):
-            early[rows, columns] = value
-        terms(0, points, store)
-
-    def d_copy(i, source=None):
-        target = lax.rem(mine + i, peers)
-        return pltpu.make_async_remote_copy(
-            src_ref=part.at[target] if source is None else source, dst_ref=rbuf.at[i], send_sem=d_send.at[i], recv_sem=d_recv.at[i],
-            device_id=(me, target), device_id_type=MESH)
-
-    @pl.when(me == 1)
-    def _():
-        pl.semaphore_wait(barrier, peers - 1)
-        pl.semaphore_signal(ready, inc=1, device_id=(0, mine), device_id_type=MESH)
-
-    @pl.when(me == 0)
-    def _():
-        pl.semaphore_wait(ready, 1)
-
-    early_terms()
-
-    @pl.when(mine != 0)
-    def _():
-        d_copy(peers - mine, early).start()
 
     planes = peers // plane
     own = mine // plane
@@ -246,14 +283,34 @@
             @pl.when(target != 0)
             def _(target=target):
                 d_copy(lax.rem(target - mine + peers, peers)).start()
-    total = part[mine]
+    @pl.when(mine == 0)
+    def _():
+        arrived = ebuf.at[pl.ds(1, 2 * peers - 1)]
+        pltpu.make_async_copy(arrived, arrived, e_recv).wait()
+        total = early[me]
+        for i in range(1, 2 * peers):
+            total = total + ebuf[i]
+        d_ref[...] = total / bands
+
+    @pl.when(mine != 0)
+    def _():
+        total = part[mine]
+        for i in range(1, peers):
+            d_copy(i).wait_recv()
+            total = total + rbuf[i]
+        d_ref[...] = total / bands
+
+    for side in range(2):
+        sends, copy = e_copy(side)
+
+        @pl.when(sends)
+        def _(copy=copy):
+            copy.wait_send()
     for i in range(1, peers):
-        d_copy(i).wait_recv()
-        total = total + rbuf[i]
-    d_ref[...] = total / bands
-
-    for i in range(1, peers):
-        d_copy(i).wait_send()
+        @pl.when(lax.rem(mine + i, peers) != 0)
+        def _(i=i):
+            d_copy(i).wait_send()
+    t_copy.wait_send()
     c_copy.wait_send()
     for copy in h_copies:
         copy.wait_send()
@@ -290,22 +347,25 @@
             pltpu.VMEM((elems, nb, half), bf16),
             pltpu.VMEM((elems, nb, half), f32),
             pltpu.VMEM((elems, nb, half), f32),
-            pltpu.VMEM((local, nb, half), bf16),
-            pltpu.VMEM((local, nb, half), bf16),
+            pltpu.VMEM((elems, nb, half), bf16),
             pltpu.VMEM((local, nb, half), bf16),
             pltpu.VMEM((local // 2, points, 2 * nb), bf16),
+            pltpu.VMEM((elems, share, nb), bf16),
             pltpu.VMEM((local // 2, 2 * nb, 2 * nb), bf16),
             pltpu.VMEM((peers, local, share), f32),
-            pltpu.VMEM((local, share), f32),
+            pltpu.VMEM((2, local, share), f32),
             pltpu.VMEM((peers, local, share), f32),
+            pltpu.VMEM((2 * peers, local, share), f32),
             pltpu.SMEM(neighbours.shape, jnp.int32),
             pltpu.SemaphoreType.REGULAR, pltpu.SemaphoreType.REGULAR,
             dma,
-            dma((2 * local + 1,)),
+            dma((2 * local + 2,)),
             dma, dma,
-            dma((local,)), dma((local,)),
+            dma((len(chunks_of(local, nb)),)), dma((len(chunks_of(local, nb)),)), dma((len(chunks_of(local, nb)),)),
+            dma, dma,
             dma, dma,
             dma((peers,)), dma((peers,)),
+            dma((2,)), dma,
         ],
         compiler_params=pltpu.CompilerParams(
             collective_id=0, has_side_effects=True, vmem_limit_bytes=grant),

time: 19.9 us -> 19.4 us (0.975)
  the two profiles are of different devices: /device:TPU:0 before, /device:TPU:1 now
where the time goes in v2:
time: 19.4 us; the launch traced here: 19.2 us
  Pallas kernels  18.6 us (96%)
  between operations  0.64 us (3%)
    pallas_call x1, Pallas kernels, quick(): pl.pallas_call(functools.partial(fused, peers, bands, plane), out_shape=(...  17.8 us
    pallas_call x1, Pallas kernels, quick(): pl.pallas_call(deliver, out_shape=(jax.ShapeDtypeStruct((local, nb, width...  0.81 us

profile of v2, /device:TPU:1, one launch (start us, length us, event | category | flops | bytes accessed | tf_op | source)
XLA Modules:
  0.0 19.2 jit_solution(4373031101772300358)
XLA Ops:
  0.6 17.8 %shard_map.59 = (bf16[4,128,512]{2,1,0:T(8,128)(2,1)S(1)}, f32[4,256]{1,0:T(4,128)S(1)}) custom-call(s32[4,27]{1,0:T(4,128)} %nb_hbm.1, bf16[4,128,512]{2,1,0:T(8,128)(2,1)} %c_hbm.1, bf16[4,27,128,128]{3,2,1,0:T(8,128)(2,1)} %h_hbm.1, bf16[4,4096,128]{2,1,0:T(8,128)(2,1)} %b_hbm.1), custom_call_target="tpu_custom_call" | custom-call | tf_op jit(solution)/shard_map/pallas_call | solution.py:337
  18.4 0.8 %shard_map.60 = (bf16[4,128,512]{2,1,0:T(8,128)(2,1)}, f32[4,256]{1,0:T(4,128)}) custom-call(bf16[4,128,512]{2,1,0:T(8,128)(2,1)S(1)} %get-tuple-element.4.f_in, f32[4,256]{1,0:T(4,128)S(1)} %get-tuple-element.5.d_in), custom_call_target="tpu_custom_call" | custom-call | tf_op jit(solution)/shard_map/pallas_call | solution.py:373

commit v3 on v2

--- a/solution.py
+++ b/solution.py
@@ -50,7 +50,7 @@
 
 
 def fused(peers, bands, plane, nb_hbm, c_hbm, h_hbm, b_hbm, f_ref, d_ref,
-          hraw, hsum, hd, y0, y1, z0, z1, fall, frecv, basis, near, gblock, part, early, rbuf, ebuf, nb_ref,
+          hraw, hsum, hd, y0, y1, z0, z1, fall, frecv, basis, near, gblock, part, early, ahead, rbuf, ebuf, nb_ref,
           hello, ready, nb_sem, load_sem, c_send, c_recv, h_load, h_send, h_recv, f_send, f_recv, t_send, t_recv,
           d_send, d_recv, e_send, e_recv):
     me = lax.axis_index("elem")
@@ -138,11 +138,15 @@
     for copy in b_loads:
         copy.start()
     t_copy = pltpu.make_async_remote_copy(
-        src_ref=b_hbm.at[:, pl.ds(0, points)], dst_ref=near.at[my_rows],
-        send_sem=t_send, recv_sem=t_recv, device_id=(other, mine), device_id_type=MESH)
-    t_copy.start()
-    n_load = pltpu.make_async_copy(b_hbm.at[:, pl.ds(0, points)], near.at[my_rows], load_sem.at[2 * local + 1])
-    n_load.start()
+        src_ref=b_hbm.at[:, pl.ds(0, points)], dst_ref=near,
+        send_sem=t_send, recv_sem=t_recv, device_id=(1, mine), device_id_type=MESH)
+    n_load = pltpu.make_async_copy(b_hbm.at[:, pl.ds(0, points)], near, load_sem.at[2 * local + 1])
+
+    @pl.when(me == 0)
+    def _():
+        t_copy.start()
+        n_load.start()
+
     c_load.wait()
     c_copy.wait_recv()
 
@@ -175,50 +179,54 @@
                 z[later][which] = following
             y[later][which] = following.astype(jnp.bfloat16)
 
-    def early_terms(side):
+    def early_terms():
         for e in range(local):
-            orbital = jnp.dot(near[side * local + e], fall[side * local + e], preferred_element_type=jnp.float32)
+            orbital = jnp.dot(near[e], fall[e], preferred_element_type=jnp.float32)
             squares = sum(orbital[:, at:at + 128] * orbital[:, at:at + 128] for at in range(0, half, 128))
             sums = jnp.sum(squares.reshape(points // 128, 128, 128), axis=2)
             for r in range(points // 128):
-                early[side, e:e + 1, r * 128:(r + 1) * 128] = sums[r:r + 1]
-
-    def e_copy(side):
-        slot = lax.rem(me + side, 2) * peers + mine
-        copy = pltpu.make_async_remote_copy(
-            src_ref=early.at[side], dst_ref=ebuf.at[slot], send_sem=e_send.at[side], recv_sem=e_recv,
-            device_id=(side, 0), device_id_type=MESH)
-        return slot != 0, copy
-
-    @pl.when(me == 1)
-    def _():
-        pl.semaphore_wait(barrier, peers - 1)
-        pl.semaphore_signal(ready, inc=1, device_id=(0, mine), device_id_type=MESH)
+                early[e:e + 1, r * 128:(r + 1) * 128] = sums[r:r + 1]
+
+    e_slot = me * peers + mine
+    e_copy = pltpu.make_async_remote_copy(
+        src_ref=early, dst_ref=ebuf.at[e_slot], send_sem=e_send, recv_sem=e_recv,
+        device_id=(0, 0), device_id_type=MESH)
 
     @pl.when(me == 0)
     def _():
-        pl.semaphore_wait(ready, 1)
-
-    t_copy.wait_recv()
-    n_load.wait()
+        n_load.wait()
+
+    @pl.when(me == 1)
+    def _():
+        t_copy.wait_recv()
+
     now, later = (CHEB - 1) % 2, CHEB % 2
     f_copy = pltpu.make_async_remote_copy(
         src_ref=fall.at[other_rows], dst_ref=frecv, send_sem=f_send, recv_sem=f_recv,
         device_id=(other, mine), device_id_type=MESH)
-    for side in range(2):
-        which = slice(side * local, (side + 1) * local)
-        fall[which] = (product(now, which, local) - z[later][which]).astype(jnp.bfloat16)
-
-        @pl.when(me != side)
+    def last_step(rows):
+        fall[rows] = (product(now, rows, local) - z[later][rows]).astype(jnp.bfloat16)
+
+    last_step(other_rows)
+    f_copy.start()
+
+    @pl.when(me == 1)
+    def _():
+        early_terms()
+        pl.semaphore_wait(barrier, peers - 1)
+        pl.semaphore_signal(ready, inc=1, device_id=(0, mine), device_id_type=MESH)
+        e_copy.start()
+
+    last_step(my_rows)
+
+    @pl.when(me == 0)
+    def _():
+        early_terms()
+        pl.semaphore_wait(ready, 1)
+
+        @pl.when(mine != 0)
         def _():
-            f_copy.start()
-
-        early_terms(side)
-        sends, copy = e_copy(side)
-
-        @pl.when(sends)
-        def _(copy=copy):
-            copy.start()
+            e_copy.start()
 
     f_ref[:, :, my_bands] = fall[my_rows]
 
@@ -249,6 +257,12 @@
                 store(column, slice(2 * pair + k, 2 * pair + k + 1),
                       slice(r * 128 - column, r * 128 - column + 128), sums[r:r + 1])
 
+    def first_terms():
+        def store(column, rows, columns, value):
+            ahead[rows, columns] = value
+        for pair in range(local // 2):
+            terms(basis[pair, pl.ds(0, points)], gblock[pair], pair, store)
+
     def group_terms(group):
         size = plane * points
         at = pl.ds(pl.multiple_of(group * size, size), size)
@@ -258,10 +272,10 @@
         for pair in range(local // 2):
             terms(basis[pair, at], gblock[pair], pair, store)
 
-    def d_copy(i):
+    def d_copy(i, source=None):
         target = lax.rem(mine + i, peers)
         return pltpu.make_async_remote_copy(
-            src_ref=part.at[target], dst_ref=rbuf.at[i], send_sem=d_send.at[i], recv_sem=d_recv.at[i],
+            src_ref=part.at[target] if source is None else source, dst_ref=rbuf.at[i], send_sem=d_send.at[i], recv_sem=d_recv.at[i],
             device_id=(me, target), device_id_type=MESH)
 
     f_copy.wait_recv()
@@ -269,6 +283,14 @@
     for e in range(local):
         at = pl.ds(e % 2 * nb, nb)
         gblock[e // 2, at, at] = (grams[e] + gram(frecv[e])).astype(jnp.bfloat16)
+
+    @pl.when(me == 1)
+    def _():
+        first_terms()
+
+        @pl.when(mine != 0)
+        def _():
+            d_copy(peers - mine, ahead).start()
 
     planes = peers // plane
     own = mine // plane
@@ -283,34 +305,33 @@
             @pl.when(target != 0)
             def _(target=target):
                 d_copy(lax.rem(target - mine + peers, peers)).start()
-    @pl.when(mine == 0)
+    @pl.when(e_slot == 0)
     def _():
         arrived = ebuf.at[pl.ds(1, 2 * peers - 1)]
         pltpu.make_async_copy(arrived, arrived, e_recv).wait()
-        total = early[me]
+        total = early[...]
         for i in range(1, 2 * peers):
             total = total + ebuf[i]
         d_ref[...] = total / bands
 
-    @pl.when(mine != 0)
+    @pl.when(e_slot != 0)
     def _():
         total = part[mine]
         for i in range(1, peers):
             d_copy(i).wait_recv()
             total = total + rbuf[i]
         d_ref[...] = total / bands
-
-    for side in range(2):
-        sends, copy = e_copy(side)
-
-        @pl.when(sends)
-        def _(copy=copy):
-            copy.wait_send()
+        e_copy.wait_send()
+
     for i in range(1, peers):
-        @pl.when(lax.rem(mine + i, peers) != 0)
+        @pl.when(lax.rem(mine + i, peers) + me != 0)
         def _(i=i):
             d_copy(i).wait_send()
-    t_copy.wait_send()
+
+    @pl.when(me == 0)
+    def _():
+        t_copy.wait_send()
+
     c_copy.wait_send()
     for copy in h_copies:
         copy.wait_send()
@@ -350,10 +371,11 @@
             pltpu.VMEM((elems, nb, half), bf16),
             pltpu.VMEM((local, nb, half), bf16),
             pltpu.VMEM((local // 2, points, 2 * nb), bf16),
-            pltpu.VMEM((elems, share, nb), bf16),
+            pltpu.VMEM((local, share, nb), bf16),
             pltpu.VMEM((local // 2, 2 * nb, 2 * nb), bf16),
             pltpu.VMEM((peers, local, share), f32),
-            pltpu.VMEM((2, local, share), f32),
+            pltpu.VMEM((local, share), f32),
+            pltpu.VMEM((local, share), f32),
             pltpu.VMEM((peers, local, share), f32),
             pltpu.VMEM((2 * peers, local, share), f32),
             pltpu.SMEM(neighbours.shape, jnp.int32),
@@ -365,7 +387,7 @@
             dma, dma,
             dma, dma,
             dma((peers,)), dma((peers,)),
-            dma((2,)), dma,
+            dma, dma,
         ],
         compiler_params=pltpu.CompilerParams(
             collective_id=0, has_side_effects=True, vmem_limit_bytes=grant),

time: 19.4 us -> 18.7 us (0.964)
  the two profiles are of different devices: /device:TPU:1 before, /device:TPU:0 now
where the time goes in v3:
time: 18.7 us; the launch traced here: 18.6 us
  Pallas kernels  17.9 us (96%)
  between operations  0.64 us (3%)
    pallas_call x1, Pallas kernels, quick(): pl.pallas_call(functools.partial(fused, peers, bands, plane), out_shape=(...  17.1 us
    pallas_call x1, Pallas kernels, quick(): pl.pallas_call(deliver, out_shape=(jax.ShapeDtypeStruct((local, nb, width...  0.81 us

profile of v3, /device:TPU:0, one launch (start us, length us, event | category | flops | bytes accessed | tf_op | source)
XLA Modules:
  0.0 18.6 jit_solution(13086523247000696860)
XLA Ops:
  0.6 17.1 %shard_map.59 = (bf16[4,128,512]{2,1,0:T(8,128)(2,1)S(1)}, f32[4,256]{1,0:T(4,128)S(1)}) custom-call(s32[4,27]{1,0:T(4,128)} %nb_hbm.1, bf16[4,128,512]{2,1,0:T(8,128)(2,1)} %c_hbm.1, bf16[4,27,128,128]{3,2,1,0:T(8,128)(2,1)} %h_hbm.1, bf16[4,4096,128]{2,1,0:T(8,128)(2,1)} %b_hbm.1), custom_call_target="tpu_custom_call" | custom-call | tf_op jit(solution)/shard_map/pallas_call | solution.py:358
  17.7 0.8 %shard_map.60 = (bf16[4,128,512]{2,1,0:T(8,128)(2,1)}, f32[4,256]{1,0:T(4,128)}) custom-call(bf16[4,128,512]{2,1,0:T(8,128)(2,1)S(1)} %get-tuple-element.4.f_in, f32[4,256]{1,0:T(4,128)S(1)} %get-tuple-element.5.d_in), custom_call_target="tpu_custom_call" | custom-call | tf_op jit(solution)/shard_map/pallas_call | solution.py:395

commit v4 on v3

--- a/solution.py
+++ b/solution.py
@@ -9,7 +9,7 @@
 
 CHEB = 6
 OFFSETS = 27
-STEP = 2
+STEP = 1
 SPLIT = 2
 MESH = pl.DeviceIdType.MESH
 
@@ -275,7 +275,7 @@
     def d_copy(i, source=None):
         target = lax.rem(mine + i, peers)
         return pltpu.make_async_remote_copy(
-            src_ref=part.at[target] if source is None else source, dst_ref=rbuf.at[i], send_sem=d_send.at[i], recv_sem=d_recv.at[i],
+            src_ref=part.at[target] if source is None else source, dst_ref=rbuf.at[i], send_sem=d_send, recv_sem=d_recv,
             device_id=(me, target), device_id_type=MESH)
 
     f_copy.wait_recv()
@@ -305,37 +305,39 @@
             @pl.when(target != 0)
             def _(target=target):
                 d_copy(lax.rem(target - mine + peers, peers)).start()
-    @pl.when(e_slot == 0)
-    def _():
-        arrived = ebuf.at[pl.ds(1, 2 * peers - 1)]
-        pltpu.make_async_copy(arrived, arrived, e_recv).wait()
-        total = early[...]
-        for i in range(1, 2 * peers):
-            total = total + ebuf[i]
-        d_ref[...] = total / bands
-
-    @pl.when(e_slot != 0)
-    def _():
-        total = part[mine]
-        for i in range(1, peers):
-            d_copy(i).wait_recv()
-            total = total + rbuf[i]
-        d_ref[...] = total / bands
-        e_copy.wait_send()
-
-    for i in range(1, peers):
-        @pl.when(lax.rem(mine + i, peers) + me != 0)
-        def _(i=i):
-            d_copy(i).wait_send()
-
-    @pl.when(me == 0)
-    def _():
-        t_copy.wait_send()
+    def wait_for(slots, sem):
+        pltpu.make_async_copy(slots, slots, sem).wait()
+
+    def added(terms):
+        while len(terms) > 1:
+            terms = [sum(terms[i:i + 2]) for i in range(0, len(terms), 2)]
+        return terms[0]
 
     c_copy.wait_send()
     for copy in h_copies:
         copy.wait_send()
     f_copy.wait_send()
+
+    @pl.when(me == 0)
+    def _():
+        t_copy.wait_send()
+
+    wait_for(rbuf.at[pl.ds(1, peers - 2)], d_send)
+
+    @pl.when((e_slot == 0) | (me == 1))
+    def _():
+        wait_for(rbuf.at[0], d_send)
+
+    @pl.when(e_slot == 0)
+    def _():
+        wait_for(ebuf.at[pl.ds(1, 2 * peers - 1)], e_recv)
+        d_ref[...] = added([early[...]] + [ebuf[i] for i in range(1, 2 * peers)]) / bands
+
+    @pl.when(e_slot != 0)
+    def _():
+        e_copy.wait_send()
+        wait_for(rbuf.at[pl.ds(1, peers - 1)], d_recv)
+        d_ref[...] = added([part[mine]] + [rbuf[i] for i in range(1, peers)]) / bands
 
 
 def deliver(f_in, d_in, f_hbm, d_hbm, sem):
@@ -386,7 +388,7 @@
             dma((len(chunks_of(local, nb)),)), dma((len(chunks_of(local, nb)),)), dma((len(chunks_of(local, nb)),)),
             dma, dma,
             dma, dma,
-            dma((peers,)), dma((peers,)),
+            dma, dma,
             dma, dma,
         ],
         compiler_params=pltpu.CompilerParams(
@@ -408,7 +410,7 @@
     def local(coefficients, hamiltonian, neighbours, basis_values):
         count, nb, width = coefficients.shape
         bands = width * peers
-        fits = (split == 2 and count * split == 8 and nb == 128 and width % 256 == 0
+        fits = (split == 2 and peers > 2 and count * split == 8 and nb == 128 and width % 256 == 0
                 and basis_values.shape[1] % (128 * peers) == 0)
         if fits:
             return quick(coefficients, hamiltonian, neighbours, basis_values, peers, bands)

time: 18.7 us -> 18.2 us (0.973)
  Pallas kernels: 17.9 us -> 17.4 us
    pallas_call x1, Pallas kernels: 17.1 us -> 16.6 us  [quick(): pl.pallas_call(functools.partial(fused, peers, bands, plane), out_shape=(...]
where the time goes in v4:
time: 18.2 us; the launch traced here: 18 us
  Pallas kernels  17.4 us (96%)
  between operations  0.64 us (4%)
    pallas_call x1, Pallas kernels, quick(): pl.pallas_call(functools.partial(fused, peers, bands, plane), out_shape=(...  16.6 us
    pallas_call x1, Pallas kernels, quick(): pl.pallas_call(deliver, out_shape=(jax.ShapeDtypeStruct((local, nb, width...  0.81 us

profile of v4, /device:TPU:0, one launch (start us, length us, event | category | flops | bytes accessed | tf_op | source)
XLA Modules:
  0.0 18.0 jit_solution(15253838701348375036)
XLA Ops:
  0.6 16.6 %shard_map.59 = (bf16[4,128,512]{2,1,0:T(8,128)(2,1)S(1)}, f32[4,256]{1,0:T(4,128)S(1)}) custom-call(s32[4,27]{1,0:T(4,128)} %nb_hbm.1, bf16[4,128,512]{2,1,0:T(8,128)(2,1)} %c_hbm.1, bf16[4,27,128,128]{3,2,1,0:T(8,128)(2,1)} %h_hbm.1, bf16[4,4096,128]{2,1,0:T(8,128)(2,1)} %b_hbm.1), custom_call_target="tpu_custom_call" | custom-call | tf_op jit(solution)/shard_map/pallas_call | solution.py:360
  17.2 0.8 %shard_map.60 = (bf16[4,128,512]{2,1,0:T(8,128)(2,1)}, f32[4,256]{1,0:T(4,128)}) custom-call(bf16[4,128,512]{2,1,0:T(8,128)(2,1)S(1)} %get-tuple-element.4.f_in, f32[4,256]{1,0:T(4,128)S(1)} %get-tuple-element.5.d_in), custom_call_target="tpu_custom_call" | custom-call | tf_op jit(solution)/shard_map/pallas_call | solution.py:397

commit v5 on v4

--- a/solution.py
+++ b/solution.py
@@ -74,9 +74,12 @@
     nb_load.start()
     for copy in loads[1:]:
         copy.start()
-    c_load = pltpu.make_async_copy(c_hbm.at[:, :, my_bands], y0.at[my_rows], load_sem.at[local])
+    c_load = pltpu.make_async_copy(c_hbm.at[:, :, my_bands], y0.at[my_rows], load_sem.at[0])
     c_load.start()
-    b_loads = [pltpu.make_async_copy(b_hbm.at[e], basis.at[e // 2, :, pl.ds(e % 2 * nb, nb)], load_sem.at[local + 1 + e]) for e in range(local)]
+    b_loads = [pltpu.make_async_copy(b_hbm.at[e], basis.at[e // 2, :, pl.ds(e % 2 * nb, nb)], load_sem.at[1]) for e in range(local)]
+
+    def wait_for(slots, sem):
+        pltpu.make_async_copy(slots, slots, sem).wait()
 
     barrier = pltpu.get_barrier_semaphore()
 
@@ -132,7 +135,7 @@
         collapse(i, e, at, rows)
         copy = pltpu.make_async_remote_copy(
             src_ref=hd.at[me * local + e, pl.ds(at, rows)], dst_ref=hd.at[me * local + e, pl.ds(at, rows)],
-            send_sem=h_send.at[i], recv_sem=h_recv.at[i], device_id=(other, mine), device_id_type=MESH)
+            send_sem=h_send, recv_sem=h_recv.at[i], device_id=(other, mine), device_id_type=MESH)
         copy.start()
         h_copies.append(copy)
     for copy in b_loads:
@@ -140,7 +143,7 @@
     t_copy = pltpu.make_async_remote_copy(
         src_ref=b_hbm.at[:, pl.ds(0, points)], dst_ref=near,
         send_sem=t_send, recv_sem=t_recv, device_id=(1, mine), device_id_type=MESH)
-    n_load = pltpu.make_async_copy(b_hbm.at[:, pl.ds(0, points)], near, load_sem.at[2 * local + 1])
+    n_load = pltpu.make_async_copy(b_hbm.at[:, pl.ds(0, points)], near, load_sem.at[2])
 
     @pl.when(me == 0)
     def _():
@@ -233,8 +236,7 @@
     def gram(block):
         return lax.dot_general(block, block, (((1,), (1,)), ((), ())), preferred_element_type=jnp.float32)
 
-    for copy in b_loads:
-        copy.wait()
+    wait_for(basis, load_sem.at[1])
     grams = [gram(fall[me * local + e]) for e in range(local)]
     gblock[...] = jnp.zeros(gblock.shape, gblock.dtype)
     pick = (lax.broadcasted_iota(jnp.int32, (8, 2 * nb), 0)
@@ -305,17 +307,13 @@
             @pl.when(target != 0)
             def _(target=target):
                 d_copy(lax.rem(target - mine + peers, peers)).start()
-    def wait_for(slots, sem):
-        pltpu.make_async_copy(slots, slots, sem).wait()
-
     def added(terms):
         while len(terms) > 1:
             terms = [sum(terms[i:i + 2]) for i in range(0, len(terms), 2)]
         return terms[0]
 
     c_copy.wait_send()
-    for copy in h_copies:
-        copy.wait_send()
+    wait_for(hd.at[my_rows], h_send)
     f_copy.wait_send()
 
     @pl.when(me == 0)
@@ -383,9 +381,9 @@
             pltpu.SMEM(neighbours.shape, jnp.int32),
             pltpu.SemaphoreType.REGULAR, pltpu.SemaphoreType.REGULAR,
             dma,
-            dma((2 * local + 2,)),
+            dma((3,)),
             dma, dma,
-            dma((len(chunks_of(local, nb)),)), dma((len(chunks_of(local, nb)),)), dma((len(chunks_of(local, nb)),)),
+            dma((len(chunks_of(local, nb)),)), dma, dma((len(chunks_of(local, nb)),)),
             dma, dma,
             dma, dma,
             dma, dma,

time: 18.2 us -> 18.1 us (level)
  no operation moved by 1% of the time
where the time goes in v5:
time: 18.1 us; the launch traced here: 17.9 us
  Pallas kernels  17.3 us (96%)
  between operations  0.64 us (4%)
    pallas_call x1, Pallas kernels, quick(): pl.pallas_call(functools.partial(fused, peers, bands, plane), out_shape=(...  16.5 us
    pallas_call x1, Pallas kernels, quick(): pl.pallas_call(deliver, out_shape=(jax.ShapeDtypeStruct((local, nb, width...  0.81 us

profile of v5, /device:TPU:0, one launch (start us, length us, event | category | flops | bytes accessed | tf_op | source)
XLA Modules:
  0.0 17.9 jit_solution(13154657131925963880)
XLA Ops:
  0.6 16.5 %shard_map.59 = (bf16[4,128,512]{2,1,0:T(8,128)(2,1)S(1)}, f32[4,256]{1,0:T(4,128)S(1)}) custom-call(s32[4,27]{1,0:T(4,128)} %nb_hbm.1, bf16[4,128,512]{2,1,0:T(8,128)(2,1)} %c_hbm.1, bf16[4,27,128,128]{3,2,1,0:T(8,128)(2,1)} %h_hbm.1, bf16[4,4096,128]{2,1,0:T(8,128)(2,1)} %b_hbm.1), custom_call_target="tpu_custom_call" | custom-call | tf_op jit(solution)/shard_map/pallas_call | solution.py:358
  17.1 0.8 %shard_map.60 = (bf16[4,128,512]{2,1,0:T(8,128)(2,1)}, f32[4,256]{1,0:T(4,128)}) custom-call(bf16[4,128,512]{2,1,0:T(8,128)(2,1)S(1)} %get-tuple-element.4.f_in, f32[4,256]{1,0:T(4,128)S(1)} %get-tuple-element.5.d_in), custom_call_target="tpu_custom_call" | custom-call | tf_op jit(solution)/shard_map/pallas_call | solution.py:395

commit v6 on v5

--- a/solution.py
+++ b/solution.py
@@ -72,10 +72,10 @@
     loads[0].start()
     nb_load = pltpu.make_async_copy(nb_hbm, nb_ref, nb_sem)
     nb_load.start()
+    c_load = pltpu.make_async_copy(c_hbm.at[:, :, my_bands], y0.at[my_rows], load_sem.at[0])
+    c_load.start()
     for copy in loads[1:]:
         copy.start()
-    c_load = pltpu.make_async_copy(c_hbm.at[:, :, my_bands], y0.at[my_rows], load_sem.at[0])
-    c_load.start()
     b_loads = [pltpu.make_async_copy(b_hbm.at[e], basis.at[e // 2, :, pl.ds(e % 2 * nb, nb)], load_sem.at[1]) for e in range(local)]
 
     def wait_for(slots, sem):

time: 18.1 us -> 18.1 us (level)
  no operation moved by 1% of the time
where the time goes in v6:
time: 18.1 us; the launch traced here: 17.9 us
  Pallas kernels  17.3 us (96%)
  between operations  0.64 us (4%)
    pallas_call x1, Pallas kernels, quick(): pl.pallas_call(functools.partial(fused, peers, bands, plane), out_shape=(...  16.5 us
    pallas_call x1, Pallas kernels, quick(): pl.pallas_call(deliver, out_shape=(jax.ShapeDtypeStruct((local, nb, width...  0.81 us

profile of v6, /device:TPU:0, one launch (start us, length us, event | category | flops | bytes accessed | tf_op | source)
XLA Modules:
  0.0 17.9 jit_solution(9878584812214457908)
XLA Ops:
  0.6 16.5 %shard_map.59 = (bf16[4,128,512]{2,1,0:T(8,128)(2,1)S(1)}, f32[4,256]{1,0:T(4,128)S(1)}) custom-call(s32[4,27]{1,0:T(4,128)} %nb_hbm.1, bf16[4,128,512]{2,1,0:T(8,128)(2,1)} %c_hbm.1, bf16[4,27,128,128]{3,2,1,0:T(8,128)(2,1)} %h_hbm.1, bf16[4,4096,128]{2,1,0:T(8,128)(2,1)} %b_hbm.1), custom_call_target="tpu_custom_call" | custom-call | tf_op jit(solution)/shard_map/pallas_call | solution.py:358
  17.1 0.8 %shard_map.60 = (bf16[4,128,512]{2,1,0:T(8,128)(2,1)}, f32[4,256]{1,0:T(4,128)}) custom-call(bf16[4,128,512]{2,1,0:T(8,128)(2,1)S(1)} %get-tuple-element.4.f_in, f32[4,256]{1,0:T(4,128)S(1)} %get-tuple-element.5.d_in), custom_call_target="tpu_custom_call" | custom-call | tf_op jit(solution)/shard_map/pallas_call | solution.py:395
